TPU v7x, 256 devices: a whole 4x4x8 slice. The times are simulated.
256 devices in a mesh: slab: 16 (over y, x), mode: 16 (over z, core).
Axes of the slice: x: 4, y: 4, z: 8, core: 2. Of those that a mesh axis runs over, the one named last changes fastest.
Arguments:
- tensor: bfloat16 [512, 131072], P('mode', 'slab'), may hold values from -24 to 24, as said below
- start_block: float32 [512, 128], replicated, may hold values from -6 to 6
Outputs:
- basis_rows: float32 [512, 128], P('mode')
- core_coeffs: float32 [131072, 128], P(('slab', 'mode'))
Inputs may be any that keep to these rules, and one draw needn't show every extreme that they name: `tensor`: entries of the unfolding; each is a row factor times a column factor times a bounded random term.
All inputs are finite; a program needn't handle non-finite values.
Results may differ from a plain program's by a relative error of at most 0.0029.
Values may be sent and summed in bfloat16 or wider, within the bound.
A program may use at most 64 MiB of HBM per device.

v0:
```python
import jax
import jax.numpy as jnp
from jax import lax
from jax.sharding import PartitionSpec as P

highest = lax.Precision.HIGHEST
contract_cols = (((1,), (1,)), ((), ()))
contract_rows = (((0,), (0,)), ((), ()))


def orthonormal(image_block):
    small_gram = jnp.dot(image_block.T, image_block, precision=highest)
    factor = jnp.linalg.cholesky(small_gram)
    return lax.linalg.triangular_solve(
        factor, image_block, left_side=False, lower=True, transpose_a=True
    )


def shards(tensor, start_block):
    row_count = tensor.shape[0]
    mode_index = lax.axis_index("mode")
    regrouped = lax.all_to_all(tensor, "mode", split_axis=1, concat_axis=0, tiled=True)
    local_gram = lax.dot_general(
        regrouped, regrouped, contract_cols, preferred_element_type=jnp.float32
    )
    gram_total = lax.psum(local_gram, ("slab", "mode"))
    image_block = jnp.dot(gram_total, start_block, precision=highest)
    basis_full = orthonormal(image_block)
    basis_low = basis_full.astype(jnp.bfloat16)
    basis_rows = lax.dynamic_slice_in_dim(basis_full, mode_index * row_count, row_count, 0)
    core_coeffs = lax.dot_general(
        regrouped, basis_low, contract_rows, preferred_element_type=jnp.float32
    )
    return (basis_rows, core_coeffs)


def solution(mesh):
    placed = (P("mode", "slab"), P())
    return jax.shard_map(
        shards,
        mesh=mesh,
        in_specs=placed,
        out_specs=(P("mode", None), P(("slab", "mode"), None)),
        check_vma=False,
    )
```

profile of v0, /device:TPU:2, one launch (start us, length us, event | category | flops | bytes accessed | tf_op | source)
XLA Modules:
  0.0 326.6 jit_solution(6227881989262356702)
XLA Ops:
  7.2 0.0 copy-start
  7.2 0.0 all-reduce.2.cloned.1.call-start
  7.2 1.1 copy.16
  8.4 24.3 %all_to_all.19 = bf16[32,16,512]{2,0,1:T(8,128)(2,1)S(1)} all-to-all(bf16[32,16,512]{2,0,1:T(8,128)(2,1)S(1)} %bitcast.28), channel_id=1, replica_groups=mesh['slab'=16,'mode'=16] {'mode'}, dimensions={1} | all-to-all | bytes 1048576 | tf_op jit(solution)/shard_map/all_to_all | solution.py:22
  32.7 1.5 fusion.5
  34.2 0.0 all-reduce.2.cloned.1.call-update
  34.2 257.6 %all-reduce.2.cloned.1.call-done = f32[512,512]{1,0:T(8,128)} async-done(((f32[512,512]{1,0:T(8,128)}), f32[512,512]{1,0:T(8,128)}) %all-reduce.2.cloned.1.call-update) | async-done | bytes 1048592 | tf_op jit(solution)/shard_map/psum | solution.py:26
  291.8 0.0 copy-done
  291.9 2.2 fusion.6
  294.1 0.6 fusion.7
  294.7 0.1 copy.12
  294.8 11.7 %cholesky.16 = f32[128,128]{1,0:T(8,128)S(1)} custom-call(f32[128,128]{1,0:T(8,128)S(1)} %fusion.4), custom_call_target="Cholesky" | custom-call | tf_op jit(solution)/shard_map/jit(cholesky)/cholesky | solution.py:13
  306.5 0.6 compare_reduce_fusion
  307.2 0.7 fusion.1
  307.8 9.8 %custom-call.6 = f32[1,128,128]{1,2,0:T(8,128)S(1)} custom-call(f32[1,128,128]{2,1,0:T(8,128)S(1)} %fusion.1), custom_call_target="InvertDiagBlocksLowerTriangular" | custom-call | tf_op jit(solution)/shard_map/triangular_solve | solution.py:14
  317.6 0.4 fusion.2
  318.0 0.3 convolution_bitcast_fusion
  318.3 0.6 constant_dynamic-slice_fusion
  318.9 0.8 copy.13
  (2 shorter events, 0.0 us)
Async XLA Ops:
  7.2 284.7 %copy-start = (f32[512,128]{1,0:T(8,128)S(1)}, f32[512,128]{1,0:T(8,128)}, u32[]{:S(2)}) copy-start(f32[512,128]{1,0:T(8,128)} %param.3) | copy-start | bytes 786436
  7.2 284.7 %all-reduce.2.cloned.1.call-start = ((), (), s32[]{:S(2)}) async-start(), calls=%async_computation.1 | async-start | bytes 2097152 | tf_op jit(solution)/shard_map/psum | solution.py:26
Sparse Core Ops, SparseCore 0:
  34.3 257.4 all-reduce.1
where the time goes:
time: 327 us
  waiting for transfers between devices  258 us (79%)
  blocking collectives  24.3 us (7%)
  other arithmetic  22.9 us (7%)
  between operations  14.1 us (4%)
  matrix products  4.92 us (2%)
    psum x1, waiting for transfers between devices, shards(): gram_total = lax.psum(local_gram, ('slab', 'mode'))  258 us
    all_to_all x1, blocking collectives, shards(): lax.all_to_all(tensor, 'mode', split_axis=1, concat_axis=0, tiled=True)  24.3 us
    another operation x3, other arithmetic, orthonormal(): factor = jnp.linalg.cholesky(small_gram)  12.4 us
    another operation x2, other arithmetic, orthonormal(): lax.linalg.triangular_solve(factor, image_block, left_side=False, lower=T...  10.5 us
  transfers between devices with their start and end apart: 1, of which 1 were waited for; matrix products, arithmetic and copies ran while one was open for 0% of the time, Pallas kernels for 0%

commit v1 on v0

--- a/solution.py
+++ b/solution.py
@@ -23,7 +23,7 @@
     local_gram = lax.dot_general(
         regrouped, regrouped, contract_cols, preferred_element_type=jnp.float32
     )
-    gram_total = lax.psum(local_gram, ("slab", "mode"))
+    gram_total = lax.psum(lax.psum(local_gram, "slab"), "mode")
     image_block = jnp.dot(gram_total, start_block, precision=highest)
     basis_full = orthonormal(image_block)
     basis_low = basis_full.astype(jnp.bfloat16)

time: 327 us -> 280 us (0.86)
  waiting for transfers between devices: 258 us -> 210 us
    psum x1 -> x2, waiting for transfers between devices: 258 us -> 210 us  [shards(): gram_total = lax.psum(lax.psum(local_gram, 'slab'), 'mode')]
  transfers between devices with their start and end apart: 1 -> 2, of which waited for: 1 -> 2; matrix products, arithmetic and copies ran while one was open for 0% -> 0% of each run, Pallas kernels for 0% -> 0%
where the time goes in v1:
time: 280 us; the launch traced here: 279 us
  waiting for transfers between devices  210 us (75%)
  blocking collectives  24.3 us (9%)
  other arithmetic  22.9 us (8%)
  between operations  14.1 us (5%)
  matrix products  4.92 us (2%)
    psum x2, waiting for transfers between devices, shards(): gram_total = lax.psum(lax.psum(local_gram, 'slab'), 'mode')  210 us
    all_to_all x1, blocking collectives, shards(): lax.all_to_all(tensor, 'mode', split_axis=1, concat_axis=0, tiled=True)  24.3 us
    another operation x3, other arithmetic, orthonormal(): factor = jnp.linalg.cholesky(small_gram)  12.4 us
    another operation x2, other arithmetic, orthonormal(): lax.linalg.triangular_solve(factor, image_block, left_side=False, lower=T...  10.5 us
  transfers between devices with their start and end apart: 2, of which 2 were waited for; matrix products, arithmetic and copies ran while one was open for 0% of the time, Pallas kernels for 0%

profile of v1, /device:TPU:2, one launch (start us, length us, event | category | flops | bytes accessed | tf_op | source)
XLA Modules:
  0.0 279.2 jit_solution(15212552196799486240)
XLA Ops:
  7.2 0.0 copy-start
  7.2 0.0 all-reduce.3.cloned.1.call-start
  7.2 1.1 copy.16
  8.4 24.3 %all_to_all.19 = bf16[32,16,512]{2,0,1:T(8,128)(2,1)S(1)} all-to-all(bf16[32,16,512]{2,0,1:T(8,128)(2,1)S(1)} %bitcast.28), channel_id=1, replica_groups=mesh['slab'=16,'mode'=16] {'mode'}, dimensions={1} | all-to-all | bytes 1048576 | tf_op jit(solution)/shard_map/all_to_all | solution.py:22
  32.7 1.5 fusion.5
  34.2 0.0 all-reduce.3.cloned.1.call-update
  34.2 0.0 all-reduce.5.cloned.1.call-start
  34.2 95.6 %all-reduce.3.cloned.1.call-done = f32[512,512]{1,0:T(8,128)} async-done(((f32[512,512]{1,0:T(8,128)}), f32[512,512]{1,0:T(8,128)}) %all-reduce.3.cloned.1.call-update) | async-done | bytes 1048592 | tf_op jit(solution)/shard_map/psum | solution.py:26
  129.9 0.0 all-reduce.5.cloned.1.call-update
  129.9 114.6 %all-reduce.5.cloned.1.call-done = f32[512,512]{1,0:T(8,128)} async-done(((f32[512,512]{1,0:T(8,128)}), f32[512,512]{1,0:T(8,128)}) %all-reduce.5.cloned.1.call-update) | async-done | bytes 1048592 | tf_op jit(solution)/shard_map/psum | solution.py:26
  244.5 0.0 copy-done
  244.5 2.2 fusion.6
  246.7 0.6 fusion.7
  247.3 0.1 copy.12
  247.4 11.7 %cholesky.16 = f32[128,128]{1,0:T(8,128)S(1)} custom-call(f32[128,128]{1,0:T(8,128)S(1)} %fusion.4), custom_call_target="Cholesky" | custom-call | tf_op jit(solution)/shard_map/jit(cholesky)/cholesky | solution.py:13
  259.1 0.6 compare_reduce_fusion
  259.8 0.7 fusion.1
  260.5 9.8 %custom-call.6 = f32[1,128,128]{1,2,0:T(8,128)S(1)} custom-call(f32[1,128,128]{2,1,0:T(8,128)S(1)} %fusion.1), custom_call_target="InvertDiagBlocksLowerTriangular" | custom-call | tf_op jit(solution)/shard_map/triangular_solve | solution.py:14
  270.3 0.4 fusion.2
  270.6 0.3 convolution_bitcast_fusion
  270.9 0.6 constant_dynamic-slice_fusion
  271.5 0.8 copy.13
  (2 shorter events, 0.0 us)
Async XLA Ops:
  7.2 237.3 %copy-start = (f32[512,128]{1,0:T(8,128)S(1)}, f32[512,128]{1,0:T(8,128)}, u32[]{:S(2)}) copy-start(f32[512,128]{1,0:T(8,128)} %param.3) | copy-start | bytes 786436
  7.2 122.7 %all-reduce.3.cloned.1.call-start = ((), (), s32[]{:S(2)}) async-start(), calls=%async_computation.1 | async-start | bytes 2097152 | tf_op jit(solution)/shard_map/psum | solution.py:26
  34.2 210.3 %all-reduce.5.cloned.1.call-start = ((), (), s32[]{:S(2)}) async-start(), calls=%async_computation.2 | async-start | bytes 2097152 | tf_op jit(solution)/shard_map/psum | solution.py:26
Sparse Core Ops, SparseCore 0:
  34.3 95.5 all-reduce.2
  132.2 112.2 all-reduce.4
